TPU v7x, 32 devices: a whole 2x2x4 slice. The times are simulated.
32 devices in a mesh: mom: 8 (over z, x), tm: 4 (over y, core).
Axes of the slice: x: 2, y: 2, z: 4, core: 2. Of those that a mesh axis runs over, the one named last changes fastest.
Arguments:
- new_rows: float32 [4, 256, 16, 512], P(None, 'mom', None, 'tm'), may hold values from -9 to 9
- history: float32 [3, 2, 256, 512, 512], P(None, None, 'mom', 'tm'), may hold values from -0.25 to 0.25
- momentum_map: int32 [256], replicated, may hold values from 0 to 255, each once
- step_index: int32 [1], replicated, may hold values from 0 to 999
- history_len: int32 [1], replicated, may hold values from 256 to 512
Outputs:
- advanced_rows: float32 [4, 256, 16, 512], P(None, 'mom', None, 'tm')
Inputs may be any that keep to these rules, and one draw needn't show every extreme that they name: `momentum_map`: each number of 0 to 255 appears once.
All inputs are finite; a program needn't handle non-finite values.
Results may differ from a plain program's by a relative error of at most 0.0003.
Values sent between devices are 32-bit elements; how exact they have to be, the bound alone decides.
A program may use at most 256 MiB of HBM per device.

v0:
```python
import functools

import jax
import jax.numpy as jnp
from jax import lax
from jax.experimental import pallas as pl
from jax.experimental.pallas import tpu as pltpu
from jax.sharding import PartitionSpec as P


SIDE = 16


TIME_STEP = 0.2
COUPLING = 5.0
DRIVE_RATE = 0.3
PRECISE = lax.Precision.HIGHEST


def lattice_tables(momentum_map, side):
    mom_count = momentum_map.shape[0]
    sites = jnp.arange(mom_count, dtype=jnp.int32)
    mom_x = momentum_map // side
    mom_y = momentum_map % side
    site_x = sites // side
    site_y = sites % side
    winding = (site_x[:, None] * mom_x[None, :] + site_y[:, None] * mom_y[None, :]) % side
    phases = winding.astype(jnp.float32) * (2.0 * jnp.pi / side)
    return (jnp.cos(phases), jnp.sin(phases))


def band_energy(own_map, row_times, side):
    wave_x = (own_map // side).astype(jnp.float32) * (2.0 * jnp.pi / side)
    wave_y = (own_map % side).astype(jnp.float32) * (2.0 * jnp.pi / side)
    drift = DRIVE_RATE * row_times
    return -2.0 * (
        jnp.cos(wave_x[:, None] + drift[None, :]) + jnp.cos(wave_y[:, None] + drift[None, :])
    )


def to_sites(cosine_table, sine_table, lattice):
    mom_count = lattice.shape[1]
    paired = lattice.reshape(2, 2, mom_count, lattice.shape[2])
    parts_re = paired[:, 0]
    parts_im = paired[:, 1]

    def apply_table(table, values):
        return jnp.einsum("rk,wkc->wrc", table, values, precision=PRECISE)

    site_re = (apply_table(cosine_table, parts_re) - apply_table(sine_table, parts_im)) / mom_count
    site_im = (apply_table(cosine_table, parts_im) + apply_table(sine_table, parts_re)) / mom_count
    return jnp.stack([site_re, site_im], axis=1).reshape(4, cosine_table.shape[0], lattice.shape[2])


def from_sites(cosine_table, sine_table, lattice):
    paired = lattice.reshape(2, 2, lattice.shape[1], lattice.shape[2])
    parts_re = paired[:, 0]
    parts_im = paired[:, 1]

    def apply_table(table, values):
        return jnp.einsum("rk,wrc->wkc", table, values, precision=PRECISE)

    mom_re = apply_table(cosine_table, parts_re) + apply_table(sine_table, parts_im)
    mom_im = apply_table(cosine_table, parts_im) - apply_table(sine_table, parts_re)
    return jnp.stack([mom_re, mom_im], axis=1).reshape(4, cosine_table.shape[1], lattice.shape[2])


def bubble_term(left_re, left_im, right_re, right_im):
    square_re = left_re * left_re - left_im * left_im
    square_im = 2.0 * left_re * left_im
    factor = -COUPLING * COUPLING
    return (
        factor * (square_re * right_re + square_im * right_im),
        factor * (square_im * right_re - square_re * right_im),
    )


def bubble(lattice):
    ret_re, ret_im, less_re, less_im = (lattice[0], lattice[1], lattice[2], lattice[3])
    great_re = less_re + ret_re
    great_im = less_im + ret_im
    lesser_re, lesser_im = bubble_term(less_re, less_im, great_re, great_im)
    greater_re, greater_im = bubble_term(great_re, great_im, less_re, less_im)
    return jnp.stack([greater_re - lesser_re, greater_im - lesser_im, lesser_re, lesser_im])


def contract(energy_pair, stored_pair):
    product = jnp.einsum("akiu,bkus->abkis", energy_pair, stored_pair, precision=PRECISE)
    return (product[0, 0] - product[1, 1], product[0, 1] + product[1, 0])


def memory_integral(self_energy, history):
    ret_ret = contract(self_energy[0:2], history[0])
    ret_less = contract(self_energy[0:2], history[1])
    less_adv = contract(self_energy[2:4], history[2])
    return TIME_STEP * jnp.stack(
        [ret_ret[0], ret_ret[1], ret_less[0] + less_adv[0], ret_less[1] + less_adv[1]]
    )


def rotate(total):
    return jnp.stack([total[1], -total[0], total[3], -total[2]])


def body(new_rows, history, momentum_map, step_index, history_len):
    own_count = new_rows.shape[1]
    row_count = new_rows.shape[2]
    time_count = new_rows.shape[3]
    cosine_table, sine_table = lattice_tables(momentum_map, SIDE)
    mom_start = lax.axis_index("mom") * own_count
    own_map = lax.dynamic_slice_in_dim(momentum_map, mom_start, own_count, 0)
    time_start = lax.axis_index("tm") * time_count
    positions = time_start + jnp.arange(time_count, dtype=jnp.int32)
    memory_mask = (positions < history_len[0]).astype(jnp.float32)
    first_times = step_index[0].astype(jnp.float32) + jnp.arange(row_count, dtype=jnp.int32).astype(
        jnp.float32
    )

    def slope(estimate, offset_steps):
        band = band_energy(own_map, (first_times + offset_steps) * TIME_STEP, SIDE)
        flattened = estimate.reshape(4, own_count, row_count * time_count)
        by_site = lax.all_to_all(flattened, "mom", split_axis=2, concat_axis=1, tiled=True)
        site_energy = from_sites(
            cosine_table, sine_table, bubble(to_sites(cosine_table, sine_table, by_site))
        )
        returned = lax.all_to_all(site_energy, "mom", split_axis=1, concat_axis=2, tiled=True)
        self_energy = returned.reshape(4, own_count, row_count, time_count)
        self_energy = self_energy * memory_mask
        partial_rows = memory_integral(self_energy, history)
        integral = lax.psum_scatter(partial_rows, "tm", scatter_dimension=3, tiled=True)
        return rotate(band[None, :, :, None] * estimate + integral)

    current = new_rows
    for time_step in range(2):
        slope_now = slope(current, float(time_step))
        estimate = current + TIME_STEP * slope_now
        for corrector in range(2):
            estimate = current + 0.5 * TIME_STEP * (
                slope_now + slope(estimate, float(time_step + 1))
            )
        current = estimate
    return current


MESH = pl.DeviceIdType.MESH
CHUNKS = 4


def halves(values):
    high = values.astype(jnp.bfloat16)
    return high, (values - high.astype(jnp.float32)).astype(jnp.bfloat16)


def product(left, right):
    return jnp.dot(left, right, preferred_element_type=jnp.float32)


def triple(left_high, left_low, right):
    right_high, right_low = halves(right)
    return (
        product(left_high, right_high)
        + product(left_high, right_low)
        + product(left_low, right_high)
    )


def integral_kernel(
    mom_size,
    slots,
    state_ref,
    mask_ref,
    site_high,
    site_low,
    back_high,
    back_low,
    history_ref,
    out_ref,
    outgoing,
    gathered,
    energy,
    returned,
    partial,
    core_rows,
    chip_rows,
    stored,
    stored_sem,
    row_send,
    row_recv,
    energy_send,
    energy_recv,
    core_send,
    core_recv,
    chip_send,
    chip_recv,
):
    mom = lax.axis_index("mom")
    tm = lax.axis_index("tm")
    core = tm % 2
    chip = tm // 2
    near = chip * 2 + (1 - core)
    far = (1 - chip) * 2 + core
    _, own, rows, times = out_ref.shape
    share = rows // mom_size
    sites = gathered.shape[2]
    chunk = own // CHUNKS

    def fetch(index, slot):
        return pltpu.make_async_copy(
            history_ref.at[:, :, index], stored.at[slot], stored_sem.at[slot]
        )

    for slot in range(slots):
        fetch(slot, slot).start()

    barrier = pltpu.get_barrier_semaphore()
    for step in range(1, mom_size):
        pl.semaphore_signal(
            barrier, inc=1, device_id={"mom": (mom + step) % mom_size}, device_id_type=MESH
        )
    for peer in (near, far):
        pl.semaphore_signal(barrier, inc=1, device_id={"tm": peer}, device_id_type=MESH)

    @pl.loop(0, rows)
    def _(row):
        for part in range(4):
            outgoing[row, part] = state_ref[pl.ds(part * own * rows + row, own, stride=rows), :]

    pl.semaphore_wait(barrier, mom_size + 1)

    def row_copy(line, step):
        peer = (mom + step) % mom_size
        return pltpu.make_async_remote_copy(
            src_ref=outgoing.at[peer * share + line],
            dst_ref=gathered.at[line, :, pl.ds(pl.multiple_of(mom * own, own), own), :],
            send_sem=row_send.at[line, step],
            recv_sem=row_recv.at[line, step],
            device_id={"mom": peer},
            device_id_type=MESH,
        )

    def landing(line):
        depth = 4 * own
        return pl.ds(pl.multiple_of((mom * share + line) * depth, depth), depth)

    def energy_copy(line, step):
        peer = (mom + step) % mom_size
        return pltpu.make_async_remote_copy(
            src_ref=energy.at[line, peer],
            dst_ref=returned.at[landing(line)],
            send_sem=energy_send.at[line, step],
            recv_sem=energy_recv.at[line, step],
            device_id={"mom": peer},
            device_id_type=MESH,
        )

    for line in range(share):
        for step in range(1, mom_size):
            row_copy(line, step).start()
    mine = pl.ds(pl.multiple_of(mom * own, own), own)
    for line in range(share):
        gathered[line, :, mine, :] = outgoing[mom * share + line]

    mask = mask_ref[0:1, :]

    @pl.loop(0, share)
    def _(line):
        for step in range(1, mom_size):
            row_copy(line, step).wait_recv()
        fields = []
        for pair in range(2):
            both = jnp.concatenate(
                [gathered[line, 2 * pair], gathered[line, 2 * pair + 1]], axis=1
            )
            turned = triple(site_high[...], site_low[...], both)
            fields.append((turned[:sites, :times] - turned[sites:, times:]) / sites)
            fields.append((turned[:sites, times:] + turned[sites:, :times]) / sites)
        ret_re, ret_im, less_re, less_im = fields
        great_re = less_re + ret_re
        great_im = less_im + ret_im
        lesser_re, lesser_im = bubble_term(less_re, less_im, great_re, great_im)
        greater_re, greater_im = bubble_term(great_re, great_im, less_re, less_im)
        pairs = (
            (greater_re - lesser_re, greater_im - lesser_im),
            (lesser_re, lesser_im),
        )
        for pair, (part_re, part_im) in enumerate(pairs):
            both = jnp.concatenate([part_re, part_im], axis=1)
            turned = triple(back_high[...], back_low[...], both)
            mom_re = (turned[:sites, :times] + turned[sites:, times:]) * mask
            mom_im = (turned[:sites, times:] - turned[sites:, :times]) * mask
            for part, values in ((2 * pair, mom_re), (2 * pair + 1, mom_im)):
                for peer in range(mom_size):
                    energy[line, peer, part * own : (part + 1) * own] = values[
                        peer * own : (peer + 1) * own
                    ]
        for step in range(1, mom_size):
            energy_copy(line, step).start()
        returned[landing(line)] = energy[line, mom]

    for line in range(share):
        for step in range(1, mom_size):
            energy_copy(line, step).wait_recv()

    def one_momentum(index):
        slot = index % slots
        fetch(index, slot).wait()
        ret_re, ret_im, less_re, less_im = [
            returned[pl.ds(part * own + index, rows, stride=4 * own), :] for part in range(4)
        ]

        def folded(part_re, part_im):
            return jnp.concatenate(
                [
                    jnp.concatenate([part_re, -part_im], axis=1),
                    jnp.concatenate([part_im, part_re], axis=1),
                ],
                axis=0,
            )

        def applied(high, both, kind):
            weights_high, weights_low = halves(stored[slot, kind].reshape(2 * times, -1))
            stacked = product(both, weights_high)
            return stacked[: 2 * rows] + stacked[2 * rows :] + product(high, weights_low)

        ret_high, ret_low = halves(folded(ret_re, ret_im))
        ret_both = jnp.concatenate([ret_high, ret_low], axis=0)
        less_high, less_low = halves(folded(less_re, less_im))
        less_both = jnp.concatenate([less_high, less_low], axis=0)
        ret_sum = applied(ret_high, ret_both, 0)
        less_sum = applied(ret_high, ret_both, 1) + applied(less_high, less_both, 2)
        for block in range(4):
            window = slice(block * times, (block + 1) * times)
            partial[block, index, : 2 * rows] = TIME_STEP * ret_sum[:, window]
            partial[block, index, 2 * rows :] = TIME_STEP * less_sum[:, window]

        @pl.when(index + slots < own)
        def _():
            fetch(index + slots, slot).start()

    def core_copy(piece, side):
        span = pl.ds(piece * chunk, chunk)
        return pltpu.make_async_remote_copy(
            src_ref=partial.at[2 * side + (1 - core), span],
            dst_ref=core_rows.at[side, span],
            send_sem=core_send.at[side, piece],
            recv_sem=core_recv.at[side, piece],
            device_id={"tm": near},
            device_id_type=MESH,
        )

    def chip_copy(piece):
        span = pl.ds(piece * chunk, chunk)
        return pltpu.make_async_remote_copy(
            src_ref=partial.at[2 * (1 - chip) + core, span],
            dst_ref=chip_rows.at[span],
            send_sem=chip_send.at[piece],
            recv_sem=chip_recv.at[piece],
            device_id={"tm": far},
            device_id_type=MESH,
        )

    @pl.loop(0, CHUNKS + 2)
    def _(turn):
        @pl.when(turn < CHUNKS)
        def _():
            @pl.loop(0, chunk)
            def _(inner):
                one_momentum(turn * chunk + inner)

            for side in range(2):
                core_copy(turn, side).start()

        @pl.when((turn >= 1) & (turn <= CHUNKS))
        def _():
            piece = turn - 1
            span = pl.ds(piece * chunk, chunk)
            for side in range(2):
                core_copy(piece, side).wait_recv()
                block = 2 * side + core
                partial[block, span] = partial[block, span] + core_rows[side, span]
            chip_copy(piece).start()

        @pl.when(turn >= 2)
        def _():
            piece = turn - 2
            span = pl.ds(piece * chunk, chunk)
            chip_copy(piece).wait_recv()
            total = partial[2 * chip + core, span] + chip_rows[span]
            for part in range(4):
                out_ref[part, span] = total[:, part * rows : (part + 1) * rows, :]

    for line in range(share):
        for step in range(1, mom_size):
            row_copy(line, step).wait_send()
            energy_copy(line, step).wait_send()
    for piece in range(CHUNKS):
        for side in range(2):
            core_copy(piece, side).wait_send()
        chip_copy(piece).wait_send()


def fits(mesh_sizes, new_rows):
    _, own_count, row_count, time_count = new_rows.shape
    return (
        mesh_sizes["tm"] == 4
        and row_count % mesh_sizes["mom"] == 0
        and row_count % 8 == 0
        and own_count % 8 == 0
        and time_count % 128 == 0
    )


def slope_integral(mom_size, estimate, mask_rows, tables, history):
    parts, own, rows, times = estimate.shape
    sites = own * mom_size
    full = history.shape[4]
    share = rows // mom_size
    slots = min(16, own)
    vmem = pl.BlockSpec(memory_space=pltpu.VMEM)
    dma = pltpu.SemaphoreType.DMA
    f32 = jnp.float32
    return pl.pallas_call(
        functools.partial(integral_kernel, mom_size, slots),
        out_shape=jax.ShapeDtypeStruct(estimate.shape, f32),
        in_specs=[vmem] * 6 + [pl.BlockSpec(memory_space=pl.ANY)],
        out_specs=vmem,
        scratch_shapes=[
            pltpu.VMEM((rows, parts, own, times), f32),
            pltpu.VMEM((share, parts, sites, times), f32),
            pltpu.VMEM((share, mom_size, parts * own, times), f32),
            pltpu.VMEM((rows * parts * own, times), f32),
            pltpu.VMEM((4, own, parts * rows, times), f32),
            pltpu.VMEM((2, own, parts * rows, times), f32),
            pltpu.VMEM((own, parts * rows, times), f32),
            pltpu.VMEM((slots, 3, 2, times, full), f32),
            dma((slots,)),
            dma((share, mom_size)),
            dma((share, mom_size)),
            dma((share, mom_size)),
            dma((share, mom_size)),
            dma((2, CHUNKS)),
            dma((2, CHUNKS)),
            dma((CHUNKS,)),
            dma((CHUNKS,)),
        ],
        compiler_params=pltpu.CompilerParams(
            collective_id=0, has_side_effects=True, vmem_limit_bytes=56 * 1024 * 1024
        ),
        name="slope_integral",
    )(estimate.reshape(parts * own * rows, times), mask_rows, *tables, history)


def table_halves(table):
    high = lax.reduce_precision(table, exponent_bits=8, mantissa_bits=7)
    return high.astype(jnp.bfloat16), (table - high).astype(jnp.bfloat16)


def fused_body(mom_size, new_rows, history, momentum_map, step_index, history_len):
    own_count = new_rows.shape[1]
    row_count = new_rows.shape[2]
    time_count = new_rows.shape[3]
    cosine_table, sine_table = lattice_tables(momentum_map, SIDE)
    tables = table_halves(jnp.concatenate([cosine_table, sine_table], axis=0)) + table_halves(
        jnp.concatenate([cosine_table.T, sine_table.T], axis=0)
    )
    own_map = lax.dynamic_slice_in_dim(momentum_map, lax.axis_index("mom") * own_count, own_count, 0)
    positions = lax.axis_index("tm") * time_count + jnp.arange(time_count, dtype=jnp.int32)
    memory_mask = (positions < history_len[0]).astype(jnp.float32)
    mask_rows = jnp.broadcast_to(memory_mask[None, :], (8, time_count))
    first_times = step_index[0].astype(jnp.float32) + jnp.arange(row_count, dtype=jnp.int32).astype(
        jnp.float32
    )

    def slope(estimate, offset_steps):
        band = band_energy(own_map, (first_times + offset_steps) * TIME_STEP, SIDE)
        integral = slope_integral(mom_size, estimate, mask_rows, tables, history)
        return rotate(band[None, :, :, None] * estimate + integral)

    current = new_rows
    for time_step in range(2):
        slope_now = slope(current, float(time_step))
        estimate = current + TIME_STEP * slope_now
        for corrector in range(2):
            estimate = current + 0.5 * TIME_STEP * (
                slope_now + slope(estimate, float(time_step + 1))
            )
        current = estimate
    return current


def solution(mesh):
    in_specs = (P(None, "mom", None, "tm"), P(None, None, "mom", "tm", None), P(), P(), P())
    out_specs = P(None, "mom", None, "tm")

    def dispatch(new_rows, *others):
        if fits(dict(mesh.shape), new_rows):
            return fused_body(mesh.shape["mom"], new_rows, *others)
        return body(new_rows, *others)

    return jax.shard_map(
        dispatch, mesh=mesh, in_specs=in_specs, out_specs=out_specs, check_vma=False
    )
```

profile of v0, /device:TPU:26, one launch (start us, length us, event | category | flops | bytes accessed | tf_op | source)
XLA Modules:
  0.0 510.9 jit_solution(481044678302474814)
XLA Ops:
  1.4 0.8 convert_multiply_fusion
  2.2 0.7 and_select_fusion.2
  2.9 0.6 broadcast_in_dim.2.mask_ref
  3.5 0.2 add_multiply_fusion
  3.8 0.1 copy.8
  3.8 0.1 copy.7
  4.0 2.2 fusion.17
  6.2 1.1 fusion.8
  7.3 82.7 %slope_integral.6 = f32[4,32,16,128]{3,2,1,0:T(8,128)} custom-call(f32[2048,128]{1,0:T(8,128)} %bitcast.9, f32[8,128]{1,0:T(8,128)} %broadcast_in_dim.2.mask_ref, bf16[512,256]{1,0:T(8,128)(2,1)} %get-tuple-element.34.site_high, bf16[512,256]{1,0:T(8,128)(2,1)} %get-tuple-element.33.site_low, bf16[512,256]{1,0:T(8,128)(2,1)} %get-tuple-element.44.back_high, ...), custom_call_target="tpu_custom_call" | custom-call | tf_op jit(solution)/shard_map/slope_integral/pallas_call | solution.py:422
  90.1 1.4 multiply_add_fusion.7
  91.5 0.1 fusion.30
  91.6 1.1 multiply_add_fusion.6
  92.7 81.4 %slope_integral.7 = f32[4,32,16,128]{3,2,1,0:T(8,128)} custom-call(f32[2048,128]{1,0:T(8,128)} %bitcast.10, f32[8,128]{1,0:T(8,128)} %broadcast_in_dim.2.mask_ref, bf16[512,256]{1,0:T(8,128)(2,1)} %get-tuple-element.34.site_high, bf16[512,256]{1,0:T(8,128)(2,1)} %get-tuple-element.33.site_low, bf16[512,256]{1,0:T(8,128)(2,1)} %get-tuple-element.44.back_high, ...), custom_call_target="tpu_custom_call" | custom-call | tf_op jit(solution)/shard_map/slope_integral/pallas_call | solution.py:422
  174.1 1.5 multiply_add_fusion.5
  175.5 0.1 fusion.29
  175.6 1.2 fusion.1
  176.8 80.7 %slope_integral.8 = f32[4,32,16,128]{3,2,1,0:T(8,128)} custom-call(f32[2048,128]{1,0:T(8,128)} %bitcast.13, f32[8,128]{1,0:T(8,128)} %broadcast_in_dim.2.mask_ref, bf16[512,256]{1,0:T(8,128)(2,1)} %get-tuple-element.34.site_high, bf16[512,256]{1,0:T(8,128)(2,1)} %get-tuple-element.33.site_low, bf16[512,256]{1,0:T(8,128)(2,1)} %get-tuple-element.44.back_high, ...), custom_call_target="tpu_custom_call" | custom-call | tf_op jit(solution)/shard_map/slope_integral/pallas_call | solution.py:422
  257.5 1.5 multiply_add_fusion.4
  259.0 0.1 fusion.28
  259.1 1.2 fusion.3
  260.3 80.2 %slope_integral.9 = f32[4,32,16,128]{3,2,1,0:T(8,128)} custom-call(f32[2048,128]{1,0:T(8,128)} %bitcast.14, f32[8,128]{1,0:T(8,128)} %broadcast_in_dim.2.mask_ref, bf16[512,256]{1,0:T(8,128)(2,1)} %get-tuple-element.34.site_high, bf16[512,256]{1,0:T(8,128)(2,1)} %get-tuple-element.33.site_low, bf16[512,256]{1,0:T(8,128)(2,1)} %get-tuple-element.44.back_high, ...), custom_call_target="tpu_custom_call" | custom-call | tf_op jit(solution)/shard_map/slope_integral/pallas_call | solution.py:422
  340.5 1.5 multiply_add_fusion.3
  342.0 0.1 fusion.27
  342.1 1.2 multiply_add_fusion.2
  343.4 80.5 %slope_integral.10 = f32[4,32,16,128]{3,2,1,0:T(8,128)} custom-call(f32[2048,128]{1,0:T(8,128)} %bitcast.11, f32[8,128]{1,0:T(8,128)} %broadcast_in_dim.2.mask_ref, bf16[512,256]{1,0:T(8,128)(2,1)} %get-tuple-element.34.site_high, bf16[512,256]{1,0:T(8,128)(2,1)} %get-tuple-element.33.site_low, bf16[512,256]{1,0:T(8,128)(2,1)} %get-tuple-element.44.back_high, ...), custom_call_target="tpu_custom_call" | custom-call | tf_op jit(solution)/shard_map/slope_integral/pallas_call | solution.py:422
  423.9 1.6 multiply_add_fusion.1
  425.5 0.1 fusion.26
  425.6 1.3 fusion.5
  426.9 80.8 %slope_integral.11 = f32[4,32,16,128]{3,2,1,0:T(8,128)} custom-call(f32[2048,128]{1,0:T(8,128)} %bitcast.12, f32[8,128]{1,0:T(8,128)} %broadcast_in_dim.2.mask_ref, bf16[512,256]{1,0:T(8,128)(2,1)} %get-tuple-element.34.site_high, bf16[512,256]{1,0:T(8,128)(2,1)} %get-tuple-element.33.site_low, bf16[512,256]{1,0:T(8,128)(2,1)} %get-tuple-element.44.back_high, ...), custom_call_target="tpu_custom_call" | custom-call | tf_op jit(solution)/shard_map/slope_integral/pallas_call | solution.py:422
  507.7 1.7 multiply_add_fusion
  509.4 0.1 fusion.25
  509.5 1.4 fusion.7
  (9 shorter events, 0.1 us)
Async XLA Ops:
  0.0 90.1 %copy-start = (f32[4,32,16,128]{3,2,1,0:T(8,128)S(1)}, f32[4,32,16,128]{3,2,1,0:T(8,128)}, u32[]{:S(2)}) copy-start(f32[4,32,16,128]{3,2,1,0:T(8,128)} %param.5) | copy-start | bytes 3145732
where the time goes:
time: 512 us; the launch traced here: 511 us
  Pallas kernels  486 us (95%)
  other arithmetic  22.2 us (4%)
    pallas_call x6, Pallas kernels, slope_integral(): pl.pallas_call(functools.partial(integral_kernel, mom_size, slots), out_s...  486 us

commit v1 on v0

--- a/solution.py
+++ b/solution.py
@@ -143,7 +143,6 @@
 
 
 MESH = pl.DeviceIdType.MESH
-CHUNKS = 4
 
 
 def halves(values):
@@ -164,17 +163,26 @@
     )
 
 
-def integral_kernel(
+STEPS = 2
+CORRECTORS = 2
+CORE_LAG = 1
+CHIP_LAG = 3
+
+
+def steps_kernel(
     mom_size,
     slots,
     state_ref,
+    band_ref,
     mask_ref,
     site_high,
     site_low,
     back_high,
     back_low,
     history_ref,
-    out_ref,
+    now,
+    base,
+    first_slope,
     outgoing,
     gathered,
     energy,
@@ -199,18 +207,24 @@
     chip = tm // 2
     near = chip * 2 + (1 - core)
     far = (1 - chip) * 2 + core
-    _, own, rows, times = out_ref.shape
-    share = rows // mom_size
-    sites = gathered.shape[2]
-    chunk = own // CHUNKS
-
-    def fetch(index, slot):
+    groups, _, pieces, _, chunk, times = outgoing.shape
+    own = pieces * chunk
+    rows = groups * mom_size
+    sites = own * mom_size
+    turns = groups * pieces
+    stages = CORRECTORS + 1
+    rounds = STEPS * stages
+    fetches = rounds * groups * own
+
+    def fetch(count):
+        slot = count % slots
         return pltpu.make_async_copy(
-            history_ref.at[:, :, index], stored.at[slot], stored_sem.at[slot]
-        )
-
-    for slot in range(slots):
-        fetch(slot, slot).start()
+            history_ref.at[:, :, count % own], stored.at[slot], stored_sem.at[slot]
+        )
+
+    @pl.loop(0, slots)
+    def _(count):
+        fetch(count).start()
 
     barrier = pltpu.get_barrier_semaphore()
     for step in range(1, mom_size):
@@ -220,56 +234,97 @@
     for peer in (near, far):
         pl.semaphore_signal(barrier, inc=1, device_id={"tm": peer}, device_id_type=MESH)
 
-    @pl.loop(0, rows)
-    def _(row):
+    def peer_of(step):
+        return (mom + step) % mom_size
+
+    def row_copy(group, piece, step):
+        return pltpu.make_async_remote_copy(
+            src_ref=outgoing.at[group, peer_of(step), piece],
+            dst_ref=gathered.at[group, mom, piece],
+            send_sem=row_send.at[group, step],
+            recv_sem=row_recv.at[group, step],
+            device_id={"mom": peer_of(step)},
+            device_id_type=MESH,
+        )
+
+    def all_rows(group, step):
+        return pltpu.make_async_remote_copy(
+            src_ref=outgoing.at[group, peer_of(step)],
+            dst_ref=gathered.at[group, mom],
+            send_sem=row_send.at[group, step],
+            recv_sem=row_recv.at[group, step],
+            device_id={"mom": peer_of(step)},
+            device_id_type=MESH,
+        )
+
+    def landing(group, piece):
+        depth = 4 * chunk
+        start = ((group * pieces + piece) * mom_size + mom) * depth
+        return pl.ds(pl.multiple_of(start, depth), depth)
+
+    def energy_copy(group, piece, step):
+        return pltpu.make_async_remote_copy(
+            src_ref=energy.at[group, peer_of(step), piece],
+            dst_ref=returned.at[landing(group, piece)],
+            send_sem=energy_send.at[group, piece, step],
+            recv_sem=energy_recv.at[group, piece, step],
+            device_id={"mom": peer_of(step)},
+            device_id_type=MESH,
+        )
+
+    def core_copy(parity, turn):
+        return pltpu.make_async_remote_copy(
+            src_ref=partial.at[turn, :, 1 - core],
+            dst_ref=core_rows.at[parity, turn],
+            send_sem=core_send.at[turn],
+            recv_sem=core_recv.at[parity, turn],
+            device_id={"tm": near},
+            device_id_type=MESH,
+        )
+
+    def chip_copy(parity, turn):
+        return pltpu.make_async_remote_copy(
+            src_ref=partial.at[turn, 1 - chip, core],
+            dst_ref=chip_rows.at[parity, turn],
+            send_sem=chip_send.at[turn],
+            recv_sem=chip_recv.at[parity, turn],
+            device_id={"tm": far},
+            device_id_type=MESH,
+        )
+
+    def publish(group, piece):
         for part in range(4):
-            outgoing[row, part] = state_ref[pl.ds(part * own * rows + row, own, stride=rows), :]
+            for row in range(mom_size):
+                start = (part * own + piece * chunk) * rows + group * mom_size + row
+                outgoing[group, row, piece, part] = now[pl.ds(start, chunk, stride=rows), :]
+        gathered[group, mom, piece] = outgoing[group, mom, piece]
+
+    def send_rows(group, piece):
+        for step in range(1, mom_size):
+            row_copy(group, piece, step).start()
+
+    now[...] = state_ref[...]
+
+    @pl.loop(0, turns)
+    def _(turn):
+        publish(turn // pieces, turn % pieces)
 
     pl.semaphore_wait(barrier, mom_size + 1)
 
-    def row_copy(line, step):
-        peer = (mom + step) % mom_size
-        return pltpu.make_async_remote_copy(
-            src_ref=outgoing.at[peer * share + line],
-            dst_ref=gathered.at[line, :, pl.ds(pl.multiple_of(mom * own, own), own), :],
-            send_sem=row_send.at[line, step],
-            recv_sem=row_recv.at[line, step],
-            device_id={"mom": peer},
-            device_id_type=MESH,
-        )
-
-    def landing(line):
-        depth = 4 * own
-        return pl.ds(pl.multiple_of((mom * share + line) * depth, depth), depth)
-
-    def energy_copy(line, step):
-        peer = (mom + step) % mom_size
-        return pltpu.make_async_remote_copy(
-            src_ref=energy.at[line, peer],
-            dst_ref=returned.at[landing(line)],
-            send_sem=energy_send.at[line, step],
-            recv_sem=energy_recv.at[line, step],
-            device_id={"mom": peer},
-            device_id_type=MESH,
-        )
-
-    for line in range(share):
+    @pl.loop(0, turns)
+    def _(turn):
+        send_rows(turn // pieces, turn % pieces)
+
+    mask = mask_ref[0:1, :]
+
+    def site_stage(group):
         for step in range(1, mom_size):
-            row_copy(line, step).start()
-    mine = pl.ds(pl.multiple_of(mom * own, own), own)
-    for line in range(share):
-        gathered[line, :, mine, :] = outgoing[mom * share + line]
-
-    mask = mask_ref[0:1, :]
-
-    @pl.loop(0, share)
-    def _(line):
-        for step in range(1, mom_size):
-            row_copy(line, step).wait_recv()
+            all_rows(group, step).wait_recv()
         fields = []
         for pair in range(2):
             both = jnp.concatenate(
-                [gathered[line, 2 * pair], gathered[line, 2 * pair + 1]], axis=1
+                [gathered[group, :, :, 2 * pair + part].reshape(sites, times) for part in range(2)],
+                axis=1,
             )
             turned = triple(site_high[...], site_low[...], both)
             fields.append((turned[:sites, :times] - turned[sites:, times:]) / sites)
@@ -289,24 +344,27 @@
             mom_re = (turned[:sites, :times] + turned[sites:, times:]) * mask
             mom_im = (turned[:sites, times:] - turned[sites:, :times]) * mask
             for part, values in ((2 * pair, mom_re), (2 * pair + 1, mom_im)):
-                for peer in range(mom_size):
-                    energy[line, peer, part * own : (part + 1) * own] = values[
-                        peer * own : (peer + 1) * own
-                    ]
+                window = pl.ds(part * chunk, chunk)
+                energy[group, :, :, window] = values.reshape(mom_size, pieces, chunk, times)
+
+        @pl.loop(0, pieces)
+        def _(piece):
+            for step in range(1, mom_size):
+                energy_copy(group, piece, step).start()
+            returned[landing(group, piece)] = energy[group, mom, piece]
+
         for step in range(1, mom_size):
-            energy_copy(line, step).start()
-        returned[landing(line)] = energy[line, mom]
-
-    for line in range(share):
-        for step in range(1, mom_size):
-            energy_copy(line, step).wait_recv()
-
-    def one_momentum(index):
-        slot = index % slots
-        fetch(index, slot).wait()
+            all_rows(group, step).wait_send()
+
+    def one_momentum(count, turn, inner):
+        slot = count % slots
+        fetch(count).wait()
+        depth = 4 * chunk
+        start = turn * mom_size * depth + inner
         ret_re, ret_im, less_re, less_im = [
-            returned[pl.ds(part * own + index, rows, stride=4 * own), :] for part in range(4)
+            returned[pl.ds(start + part * chunk, mom_size, stride=depth), :] for part in range(4)
         ]
+        lines = 2 * mom_size
 
         def folded(part_re, part_im):
             return jnp.concatenate(
@@ -320,7 +378,7 @@
         def applied(high, both, kind):
             weights_high, weights_low = halves(stored[slot, kind].reshape(2 * times, -1))
             stacked = product(both, weights_high)
-            return stacked[: 2 * rows] + stacked[2 * rows :] + product(high, weights_low)
+            return stacked[:lines] + stacked[lines:] + product(high, weights_low)
 
         ret_high, ret_low = halves(folded(ret_re, ret_im))
         ret_both = jnp.concatenate([ret_high, ret_low], axis=0)
@@ -330,124 +388,159 @@
         less_sum = applied(ret_high, ret_both, 1) + applied(less_high, less_both, 2)
         for block in range(4):
             window = slice(block * times, (block + 1) * times)
-            partial[block, index, : 2 * rows] = TIME_STEP * ret_sum[:, window]
-            partial[block, index, 2 * rows :] = TIME_STEP * less_sum[:, window]
-
-        @pl.when(index + slots < own)
+            partial[turn, block // 2, block % 2, inner, :lines] = ret_sum[:, window]
+            partial[turn, block // 2, block % 2, inner, lines:] = less_sum[:, window]
+
+        @pl.when(count + slots < fetches)
         def _():
-            fetch(index + slots, slot).start()
-
-    def core_copy(piece, side):
-        span = pl.ds(piece * chunk, chunk)
-        return pltpu.make_async_remote_copy(
-            src_ref=partial.at[2 * side + (1 - core), span],
-            dst_ref=core_rows.at[side, span],
-            send_sem=core_send.at[side, piece],
-            recv_sem=core_recv.at[side, piece],
-            device_id={"tm": near},
-            device_id_type=MESH,
-        )
-
-    def chip_copy(piece):
-        span = pl.ds(piece * chunk, chunk)
-        return pltpu.make_async_remote_copy(
-            src_ref=partial.at[2 * (1 - chip) + core, span],
-            dst_ref=chip_rows.at[span],
-            send_sem=chip_send.at[piece],
-            recv_sem=chip_recv.at[piece],
-            device_id={"tm": far},
-            device_id_type=MESH,
-        )
-
-    @pl.loop(0, CHUNKS + 2)
-    def _(turn):
-        @pl.when(turn < CHUNKS)
-        def _():
-            @pl.loop(0, chunk)
-            def _(inner):
-                one_momentum(turn * chunk + inner)
-
-            for side in range(2):
-                core_copy(turn, side).start()
-
-        @pl.when((turn >= 1) & (turn <= CHUNKS))
-        def _():
-            piece = turn - 1
-            span = pl.ds(piece * chunk, chunk)
-            for side in range(2):
-                core_copy(piece, side).wait_recv()
-                block = 2 * side + core
-                partial[block, span] = partial[block, span] + core_rows[side, span]
-            chip_copy(piece).start()
-
-        @pl.when(turn >= 2)
-        def _():
-            piece = turn - 2
-            span = pl.ds(piece * chunk, chunk)
-            chip_copy(piece).wait_recv()
-            total = partial[2 * chip + core, span] + chip_rows[span]
-            for part in range(4):
-                out_ref[part, span] = total[:, part * rows : (part + 1) * rows, :]
-
-    for line in range(share):
-        for step in range(1, mom_size):
-            row_copy(line, step).wait_send()
-            energy_copy(line, step).wait_send()
-    for piece in range(CHUNKS):
-        for side in range(2):
-            core_copy(piece, side).wait_send()
-        chip_copy(piece).wait_send()
+            fetch(count + slots).start()
+
+    def update(parity, turn, inner, moment, first):
+        group = turn // pieces
+        index = (turn % pieces) * chunk + inner
+        total = (
+            partial[turn, chip, core, inner]
+            + core_rows[parity, turn, chip, inner]
+            + chip_rows[parity, turn, inner]
+        )
+        span = [
+            pl.ds(
+                pl.multiple_of((part * own + index) * rows + group * mom_size, mom_size), mom_size
+            )
+            for part in range(4)
+        ]
+        band = band_ref[
+            pl.ds(
+                pl.multiple_of((moment * own + index) * rows + group * mom_size, mom_size), mom_size
+            ),
+            :,
+        ]
+        terms = [
+            band * now[span[part], :] + TIME_STEP * total[part * mom_size : (part + 1) * mom_size]
+            for part in range(4)
+        ]
+        slopes = (terms[1], -terms[0], terms[3], -terms[2])
+        for part in range(4):
+            start = jnp.where(first, now[span[part], :], base[span[part], :])
+            early = jnp.where(first, slopes[part], first_slope[span[part], :])
+            base[span[part], :] = start
+            first_slope[span[part], :] = early
+            now[span[part], :] = start + 0.5 * TIME_STEP * (early + slopes[part])
+
+    @pl.loop(0, rounds)
+    def _(count):
+        parity = count % 2
+        stage = count % stages
+        first = stage == 0
+        moment = count // stages + jnp.minimum(stage, 1)
+
+        @pl.loop(0, groups)
+        def _(group):
+            site_stage(group)
+
+        @pl.loop(0, turns + CHIP_LAG)
+        def _(turn):
+            @pl.when(turn < turns)
+            def _():
+                for step in range(1, mom_size):
+                    energy_copy(turn // pieces, turn % pieces, step).wait_recv()
+
+                @pl.loop(0, chunk // 2)
+                def _(couple):
+                    for inner in range(2):
+                        index = 2 * couple + inner
+                        one_momentum((count * turns + turn) * chunk + index, turn, index)
+
+                core_copy(parity, turn).start()
+
+            @pl.when((turn >= CORE_LAG) & (turn < turns + CORE_LAG))
+            def _():
+                ready = turn - CORE_LAG
+                core_copy(parity, ready).wait_recv()
+                partial[ready, 1 - chip, core] = (
+                    partial[ready, 1 - chip, core] + core_rows[parity, ready, 1 - chip]
+                )
+                chip_copy(parity, ready).start()
+
+            @pl.when(turn >= CHIP_LAG)
+            def _():
+                ready = turn - CHIP_LAG
+                chip_copy(parity, ready).wait_recv()
+
+                @pl.loop(0, chunk)
+                def _(inner):
+                    update(parity, ready, inner, moment, first)
+
+                @pl.when(count + 1 < rounds)
+                def _():
+                    publish(ready // pieces, ready % pieces)
+                    send_rows(ready // pieces, ready % pieces)
+
+                core_copy(parity, ready).wait_send()
+                chip_copy(parity, ready).wait_send()
+
+        @pl.loop(0, turns)
+        def _(turn):
+            for step in range(1, mom_size):
+                energy_copy(turn // pieces, turn % pieces, step).wait_send()
 
 
 def fits(mesh_sizes, new_rows):
     _, own_count, row_count, time_count = new_rows.shape
     return (
         mesh_sizes["tm"] == 4
+        and mesh_sizes["mom"] % 8 == 0
         and row_count % mesh_sizes["mom"] == 0
-        and row_count % 8 == 0
         and own_count % 8 == 0
         and time_count % 128 == 0
     )
 
 
-def slope_integral(mom_size, estimate, mask_rows, tables, history):
-    parts, own, rows, times = estimate.shape
-    sites = own * mom_size
+def advance(mom_size, new_rows, bands, mask_rows, tables, history):
+    parts, own, rows, times = new_rows.shape
     full = history.shape[4]
-    share = rows // mom_size
+    groups = rows // mom_size
+    chunk = 8
+    pieces = own // chunk
+    turns = groups * pieces
     slots = min(16, own)
+    lines = parts * mom_size
     vmem = pl.BlockSpec(memory_space=pltpu.VMEM)
     dma = pltpu.SemaphoreType.DMA
     f32 = jnp.float32
-    return pl.pallas_call(
-        functools.partial(integral_kernel, mom_size, slots),
-        out_shape=jax.ShapeDtypeStruct(estimate.shape, f32),
-        in_specs=[vmem] * 6 + [pl.BlockSpec(memory_space=pl.ANY)],
+    flat = (parts * own * rows, times)
+    result = pl.pallas_call(
+        functools.partial(steps_kernel, mom_size, slots),
+        out_shape=jax.ShapeDtypeStruct(flat, f32),
+        in_specs=[vmem] * 7 + [pl.BlockSpec(memory_space=pl.ANY)],
         out_specs=vmem,
         scratch_shapes=[
-            pltpu.VMEM((rows, parts, own, times), f32),
-            pltpu.VMEM((share, parts, sites, times), f32),
-            pltpu.VMEM((share, mom_size, parts * own, times), f32),
-            pltpu.VMEM((rows * parts * own, times), f32),
-            pltpu.VMEM((4, own, parts * rows, times), f32),
-            pltpu.VMEM((2, own, parts * rows, times), f32),
-            pltpu.VMEM((own, parts * rows, times), f32),
+            pltpu.VMEM(flat, f32),
+            pltpu.VMEM(flat, f32),
+            pltpu.VMEM((groups, mom_size, pieces, parts, chunk, times), f32),
+            pltpu.VMEM((groups, mom_size, pieces, parts, chunk, times), f32),
+            pltpu.VMEM((groups, mom_size, pieces, parts * chunk, times), f32),
+            pltpu.VMEM((turns * mom_size * parts * chunk, times), f32),
+            pltpu.VMEM((turns, 2, 2, chunk, lines, times), f32),
+            pltpu.VMEM((2, turns, 2, chunk, lines, times), f32),
+            pltpu.VMEM((2, turns, chunk, lines, times), f32),
             pltpu.VMEM((slots, 3, 2, times, full), f32),
             dma((slots,)),
-            dma((share, mom_size)),
-            dma((share, mom_size)),
-            dma((share, mom_size)),
-            dma((share, mom_size)),
-            dma((2, CHUNKS)),
-            dma((2, CHUNKS)),
-            dma((CHUNKS,)),
-            dma((CHUNKS,)),
+            dma((groups, mom_size)),
+            dma((groups, mom_size)),
+            dma((groups, pieces, mom_size)),
+            dma((groups, pieces, mom_size)),
+            dma((turns,)),
+            dma((2, turns)),
+            dma((turns,)),
+            dma((2, turns)),
         ],
         compiler_params=pltpu.CompilerParams(
-            collective_id=0, has_side_effects=True, vmem_limit_bytes=56 * 1024 * 1024
+            collective_id=0, has_side_effects=True, vmem_limit_bytes=60 * 1024 * 1024
         ),
-        name="slope_integral",
-    )(estimate.reshape(parts * own * rows, times), mask_rows, *tables, history)
+        name="advance_rows",
+    )(new_rows.reshape(flat), bands, mask_rows, *tables, history)
+    return result.reshape(new_rows.shape)
 
 
 def table_halves(table):
@@ -470,22 +563,14 @@
     first_times = step_index[0].astype(jnp.float32) + jnp.arange(row_count, dtype=jnp.int32).astype(
         jnp.float32
     )
-
-    def slope(estimate, offset_steps):
-        band = band_energy(own_map, (first_times + offset_steps) * TIME_STEP, SIDE)
-        integral = slope_integral(mom_size, estimate, mask_rows, tables, history)
-        return rotate(band[None, :, :, None] * estimate + integral)
-
-    current = new_rows
-    for time_step in range(2):
-        slope_now = slope(current, float(time_step))
-        estimate = current + TIME_STEP * slope_now
-        for corrector in range(2):
-            estimate = current + 0.5 * TIME_STEP * (
-                slope_now + slope(estimate, float(time_step + 1))
-            )
-        current = estimate
-    return current
+    bands = jnp.stack(
+        [
+            band_energy(own_map, (first_times + float(offset)) * TIME_STEP, SIDE)
+            for offset in range(STEPS + 1)
+        ]
+    )
+    bands = jnp.broadcast_to(bands.reshape(-1, 1), (bands.size, time_count))
+    return advance(mom_size, new_rows, bands, mask_rows, tables, history)
 
 
 def solution(mesh):

time: 512 us -> 319 us (0.62)
  Pallas kernels: 486 us -> 308 us
  other arithmetic: 22.2 us -> 5.07 us
    pallas_call x6 -> x1, Pallas kernels: 486 us -> 308 us  [advance(): pl.pallas_call(functools.partial(steps_kernel, mom_size, slots), out_shap...]
    add x12 -> x0, other arithmetic: 16.6 us -> none  [the longest x6 9.2 us: slope(): return rotate(band[None, :, :, None] * estimate + integral)]
where the time goes in v1:
time: 319 us
  Pallas kernels  308 us (97%)
  other arithmetic  5.07 us (2%)
  local copies, waits for them, and re-layouts  4.2 us (1%)
    pallas_call x1, Pallas kernels, advance(): pl.pallas_call(functools.partial(steps_kernel, mom_size, slots), out_shap...  308 us

profile of v1, /device:TPU:26, one launch (start us, length us, event | category | flops | bytes accessed | tf_op | source)
XLA Modules:
  0.0 318.9 jit_solution(10384711615212083769)
XLA Ops:
  0.0 0.8 convert_multiply_fusion
  1.4 0.2 add_multiply_fusion.2
  1.7 0.1 copy.6
  1.8 0.1 broadcast_in_dim.6
  1.9 1.2 broadcast_in_dim.7.band_ref
  3.0 0.7 and_select_fusion.2
  3.7 2.2 fusion.9
  6.0 1.1 fusion
  7.7 0.6 broadcast_in_dim.8.mask_ref
  8.3 308.2 %advance_rows.1 = f32[2048,128]{1,0:T(8,128)} custom-call(f32[2048,128]{1,0:T(8,128)} %bitcast.6, f32[1536,128]{1,0:T(8,128)} %broadcast_in_dim.7.band_ref, f32[8,128]{1,0:T(8,128)} %broadcast_in_dim.8.mask_ref, bf16[512,256]{1,0:T(8,128)(2,1)} %get-tuple-element.10.site_high, bf16[512,256]{1,0:T(8,128)(2,1)} %get-tuple-element.9.site_low, ...), custom_call_target="tpu_custom_call" | custom-call | tf_op jit(solution)/shard_map/advance_rows/pallas_call | solution.py:512
  316.6 2.3 copy.10
  (7 shorter events, 0.0 us)

commit v2 on v1

--- a/solution.py
+++ b/solution.py
@@ -167,18 +167,17 @@
 CORRECTORS = 2
 CORE_LAG = 1
 CHIP_LAG = 3
+DEPTH = CHIP_LAG + 1
+UNROLL = 4
+RING = 4
 
 
 def steps_kernel(
     mom_size,
-    slots,
+    map_ref,
+    step_ref,
+    length_ref,
     state_ref,
-    band_ref,
-    mask_ref,
-    site_high,
-    site_low,
-    back_high,
-    back_low,
     history_ref,
     now,
     base,
@@ -191,6 +190,13 @@
     core_rows,
     chip_rows,
     stored,
+    site_high,
+    site_low,
+    back_high,
+    back_low,
+    own_waves,
+    time_waves,
+    state_sem,
     stored_sem,
     row_send,
     row_recv,
@@ -214,17 +220,23 @@
     turns = groups * pieces
     stages = CORRECTORS + 1
     rounds = STEPS * stages
-    fetches = rounds * groups * own
+    quads = own // UNROLL
+    resident = own - quads
+    fetches = rounds * groups * quads
+
+    def load(index, slot):
+        return pltpu.make_async_copy(
+            history_ref.at[:, :, index], stored.at[slot], stored_sem.at[slot]
+        )
+
+    def keep(quad, place):
+        return load(quad * UNROLL + place, quad * (UNROLL - 1) + place)
 
     def fetch(count):
-        slot = count % slots
-        return pltpu.make_async_copy(
-            history_ref.at[:, :, count % own], stored.at[slot], stored_sem.at[slot]
-        )
-
-    @pl.loop(0, slots)
-    def _(count):
-        fetch(count).start()
+        return load(count % quads * UNROLL + UNROLL - 1, resident + count % RING)
+
+    state_copy = pltpu.make_async_copy(state_ref, now, state_sem)
+    state_copy.start()
 
     barrier = pltpu.get_barrier_semaphore()
     for step in range(1, mom_size):
@@ -272,22 +284,22 @@
             device_id_type=MESH,
         )
 
-    def core_copy(parity, turn):
+    def core_copy(turn):
         return pltpu.make_async_remote_copy(
-            src_ref=partial.at[turn, :, 1 - core],
-            dst_ref=core_rows.at[parity, turn],
+            src_ref=partial.at[turn % DEPTH, :, 1 - core],
+            dst_ref=core_rows.at[turn],
             send_sem=core_send.at[turn],
-            recv_sem=core_recv.at[parity, turn],
+            recv_sem=core_recv.at[turn],
             device_id={"tm": near},
             device_id_type=MESH,
         )
 
-    def chip_copy(parity, turn):
+    def chip_copy(turn):
         return pltpu.make_async_remote_copy(
-            src_ref=partial.at[turn, 1 - chip, core],
-            dst_ref=chip_rows.at[parity, turn],
+            src_ref=partial.at[turn % DEPTH, 1 - chip, core],
+            dst_ref=chip_rows.at[turn],
             send_sem=chip_send.at[turn],
-            recv_sem=chip_recv.at[parity, turn],
+            recv_sem=chip_recv.at[turn],
             device_id={"tm": far},
             device_id_type=MESH,
         )
@@ -303,19 +315,52 @@
         for step in range(1, mom_size):
             row_copy(group, piece, step).start()
 
-    now[...] = state_ref[...]
+    state_copy.wait()
+    pl.semaphore_wait(barrier, mom_size + 1)
 
     @pl.loop(0, turns)
     def _(turn):
         publish(turn // pieces, turn % pieces)
-
-    pl.semaphore_wait(barrier, mom_size + 1)
-
-    @pl.loop(0, turns)
-    def _(turn):
         send_rows(turn // pieces, turn % pieces)
 
-    mask = mask_ref[0:1, :]
+    @pl.loop(0, quads)
+    def _(quad):
+        for place in range(UNROLL - 1):
+            keep(quad, place).start()
+
+        @pl.when(quad < RING)
+        def _():
+            fetch(quad).start()
+
+    square = (sites, sites)
+    turn_of = 2.0 * jnp.pi / SIDE
+    place_row = jnp.broadcast_to(map_ref[0:1, :], square)
+    place_column = jnp.transpose(place_row.astype(jnp.float32)).astype(jnp.int32)
+
+    def table_of(first, second, high_ref, low_ref):
+        winding = (first // SIDE) * (second // SIDE) + (first % SIDE) * (second % SIDE)
+        phases = (winding % SIDE).astype(jnp.float32) * turn_of
+        for half, values in enumerate((jnp.cos(phases), jnp.sin(phases))):
+            high, low = halves(values)
+            high_ref[half * sites : (half + 1) * sites] = high
+            low_ref[half * sites : (half + 1) * sites] = low
+
+    table_of(lax.broadcasted_iota(jnp.int32, square, 0), place_row, site_high, site_low)
+    table_of(place_column, lax.broadcasted_iota(jnp.int32, square, 1), back_high, back_low)
+
+    column = place_column[:, :times]
+    for kind, index in enumerate((column // SIDE, column % SIDE)):
+        wave = index.astype(jnp.float32) * turn_of
+        own_waves[2 * kind] = jnp.cos(wave)
+        own_waves[2 * kind + 1] = jnp.sin(wave)
+    late = (STEPS + 1) * rows
+    label = lax.broadcasted_iota(jnp.int32, (late, times), 0)
+    ahead = label % rows + label // rows
+    drift = DRIVE_RATE * ((step_ref[0] + ahead).astype(jnp.float32) * TIME_STEP)
+    time_waves[0] = jnp.cos(drift)
+    time_waves[1] = jnp.sin(drift)
+    position = tm * times + lax.broadcasted_iota(jnp.int32, (1, times), 1)
+    mask = (position < length_ref[0]).astype(jnp.float32)
 
     def site_stage(group):
         for step in range(1, mom_size):
@@ -356,9 +401,7 @@
         for step in range(1, mom_size):
             all_rows(group, step).wait_send()
 
-    def one_momentum(count, turn, inner):
-        slot = count % slots
-        fetch(count).wait()
+    def one_momentum(slot, turn, inner):
         depth = 4 * chunk
         start = turn * mom_size * depth + inner
         ret_re, ret_im, less_re, less_im = [
@@ -388,20 +431,16 @@
         less_sum = applied(ret_high, ret_both, 1) + applied(less_high, less_both, 2)
         for block in range(4):
             window = slice(block * times, (block + 1) * times)
-            partial[turn, block // 2, block % 2, inner, :lines] = ret_sum[:, window]
-            partial[turn, block // 2, block % 2, inner, lines:] = less_sum[:, window]
-
-        @pl.when(count + slots < fetches)
-        def _():
-            fetch(count + slots).start()
-
-    def update(parity, turn, inner, moment, first):
+            partial[turn % DEPTH, block // 2, block % 2, inner, :lines] = ret_sum[:, window]
+            partial[turn % DEPTH, block // 2, block % 2, inner, lines:] = less_sum[:, window]
+
+    def update(turn, inner, moment, first):
         group = turn // pieces
         index = (turn % pieces) * chunk + inner
         total = (
-            partial[turn, chip, core, inner]
-            + core_rows[parity, turn, chip, inner]
-            + chip_rows[parity, turn, inner]
+            partial[turn % DEPTH, chip, core, inner]
+            + core_rows[turn, chip, inner]
+            + chip_rows[turn, inner]
         )
         span = [
             pl.ds(
@@ -409,12 +448,12 @@
             )
             for part in range(4)
         ]
-        band = band_ref[
-            pl.ds(
-                pl.multiple_of((moment * own + index) * rows + group * mom_size, mom_size), mom_size
-            ),
-            :,
-        ]
+        instant = pl.ds(pl.multiple_of(moment * rows + group * mom_size, mom_size), mom_size)
+        wave = [own_waves[kind, pl.ds(mom * own + index, 1), :] for kind in range(4)]
+        band = -2.0 * (
+            (wave[0] + wave[2]) * time_waves[0, instant]
+            - (wave[1] + wave[3]) * time_waves[1, instant]
+        )
         terms = [
             band * now[span[part], :] + TIME_STEP * total[part * mom_size : (part + 1) * mom_size]
             for part in range(4)
@@ -429,7 +468,6 @@
 
     @pl.loop(0, rounds)
     def _(count):
-        parity = count % 2
         stage = count % stages
         first = stage == 0
         moment = count // stages + jnp.minimum(stage, 1)
@@ -445,39 +483,56 @@
                 for step in range(1, mom_size):
                     energy_copy(turn // pieces, turn % pieces, step).wait_recv()
 
-                @pl.loop(0, chunk // 2)
-                def _(couple):
-                    for inner in range(2):
-                        index = 2 * couple + inner
-                        one_momentum((count * turns + turn) * chunk + index, turn, index)
-
-                core_copy(parity, turn).start()
+                @pl.loop(0, chunk // UNROLL)
+                def _(part):
+                    quad = turn % pieces * (chunk // UNROLL) + part
+                    serial = (count * turns + turn) * (chunk // UNROLL) + part
+
+                    @pl.when((count == 0) & (turn < pieces))
+                    def _():
+                        for place in range(UNROLL - 1):
+                            keep(quad, place).wait()
+
+                    fetch(serial).wait()
+                    for place in range(UNROLL - 1):
+                        one_momentum(
+                            quad * (UNROLL - 1) + place, turn, part * UNROLL + place
+                        )
+                    one_momentum(
+                        resident + serial % RING, turn, part * UNROLL + UNROLL - 1
+                    )
+
+                    @pl.when(serial + RING < fetches)
+                    def _():
+                        fetch(serial + RING).start()
+
+                core_copy(turn).start()
 
             @pl.when((turn >= CORE_LAG) & (turn < turns + CORE_LAG))
             def _():
                 ready = turn - CORE_LAG
-                core_copy(parity, ready).wait_recv()
-                partial[ready, 1 - chip, core] = (
-                    partial[ready, 1 - chip, core] + core_rows[parity, ready, 1 - chip]
+                core_copy(ready).wait_recv()
+                partial[ready % DEPTH, 1 - chip, core] = (
+                    partial[ready % DEPTH, 1 - chip, core] + core_rows[ready, 1 - chip]
                 )
-                chip_copy(parity, ready).start()
+                chip_copy(ready).start()
 
             @pl.when(turn >= CHIP_LAG)
             def _():
                 ready = turn - CHIP_LAG
-                chip_copy(parity, ready).wait_recv()
+                chip_copy(ready).wait_recv()
 
                 @pl.loop(0, chunk)
                 def _(inner):
-                    update(parity, ready, inner, moment, first)
+                    update(ready, inner, moment, first)
 
                 @pl.when(count + 1 < rounds)
                 def _():
                     publish(ready // pieces, ready % pieces)
                     send_rows(ready // pieces, ready % pieces)
 
-                core_copy(parity, ready).wait_send()
-                chip_copy(parity, ready).wait_send()
+                core_copy(ready).wait_send()
+                chip_copy(ready).wait_send()
 
         @pl.loop(0, turns)
         def _(turn):
@@ -491,28 +546,34 @@
         mesh_sizes["tm"] == 4
         and mesh_sizes["mom"] % 8 == 0
         and row_count % mesh_sizes["mom"] == 0
+        and row_count * own_count >= 64 * mesh_sizes["mom"]
         and own_count % 8 == 0
         and time_count % 128 == 0
+        and time_count <= own_count * mesh_sizes["mom"]
     )
 
 
-def advance(mom_size, new_rows, bands, mask_rows, tables, history):
+def advance(mom_size, new_rows, history, momentum_map, step_index, history_len):
     parts, own, rows, times = new_rows.shape
     full = history.shape[4]
     groups = rows // mom_size
     chunk = 8
     pieces = own // chunk
     turns = groups * pieces
-    slots = min(16, own)
+    slots = own - own // UNROLL + RING
     lines = parts * mom_size
+    sites = own * mom_size
     vmem = pl.BlockSpec(memory_space=pltpu.VMEM)
+    smem = pl.BlockSpec(memory_space=pltpu.SMEM)
+    whole = pl.BlockSpec(memory_space=pl.ANY)
+    table = pltpu.VMEM((2 * sites, sites), jnp.bfloat16)
     dma = pltpu.SemaphoreType.DMA
     f32 = jnp.float32
     flat = (parts * own * rows, times)
     result = pl.pallas_call(
-        functools.partial(steps_kernel, mom_size, slots),
+        functools.partial(steps_kernel, mom_size),
         out_shape=jax.ShapeDtypeStruct(flat, f32),
-        in_specs=[vmem] * 7 + [pl.BlockSpec(memory_space=pl.ANY)],
+        in_specs=[vmem, smem, smem, whole, whole],
         out_specs=vmem,
         scratch_shapes=[
             pltpu.VMEM(flat, f32),
@@ -521,56 +582,33 @@
             pltpu.VMEM((groups, mom_size, pieces, parts, chunk, times), f32),
             pltpu.VMEM((groups, mom_size, pieces, parts * chunk, times), f32),
             pltpu.VMEM((turns * mom_size * parts * chunk, times), f32),
-            pltpu.VMEM((turns, 2, 2, chunk, lines, times), f32),
-            pltpu.VMEM((2, turns, 2, chunk, lines, times), f32),
-            pltpu.VMEM((2, turns, chunk, lines, times), f32),
+            pltpu.VMEM((DEPTH, 2, 2, chunk, lines, times), f32),
+            pltpu.VMEM((turns, 2, chunk, lines, times), f32),
+            pltpu.VMEM((turns, chunk, lines, times), f32),
             pltpu.VMEM((slots, 3, 2, times, full), f32),
+            table,
+            table,
+            table,
+            table,
+            pltpu.VMEM((4, sites, times), f32),
+            pltpu.VMEM((2, (STEPS + 1) * rows, times), f32),
+            dma(()),
             dma((slots,)),
             dma((groups, mom_size)),
             dma((groups, mom_size)),
             dma((groups, pieces, mom_size)),
             dma((groups, pieces, mom_size)),
             dma((turns,)),
-            dma((2, turns)),
             dma((turns,)),
-            dma((2, turns)),
+            dma((turns,)),
+            dma((turns,)),
         ],
         compiler_params=pltpu.CompilerParams(
-            collective_id=0, has_side_effects=True, vmem_limit_bytes=60 * 1024 * 1024
+            collective_id=0, has_side_effects=True, vmem_limit_bytes=63 * 1024 * 1024
         ),
         name="advance_rows",
-    )(new_rows.reshape(flat), bands, mask_rows, *tables, history)
+    )(momentum_map.reshape(1, -1), step_index, history_len, new_rows.reshape(flat), history)
     return result.reshape(new_rows.shape)
-
-
-def table_halves(table):
-    high = lax.reduce_precision(table, exponent_bits=8, mantissa_bits=7)
-    return high.astype(jnp.bfloat16), (table - high).astype(jnp.bfloat16)
-
-
-def fused_body(mom_size, new_rows, history, momentum_map, step_index, history_len):
-    own_count = new_rows.shape[1]
-    row_count = new_rows.shape[2]
-    time_count = new_rows.shape[3]
-    cosine_table, sine_table = lattice_tables(momentum_map, SIDE)
-    tables = table_halves(jnp.concatenate([cosine_table, sine_table], axis=0)) + table_halves(
-        jnp.concatenate([cosine_table.T, sine_table.T], axis=0)
-    )
-    own_map = lax.dynamic_slice_in_dim(momentum_map, lax.axis_index("mom") * own_count, own_count, 0)
-    positions = lax.axis_index("tm") * time_count + jnp.arange(time_count, dtype=jnp.int32)
-    memory_mask = (positions < history_len[0]).astype(jnp.float32)
-    mask_rows = jnp.broadcast_to(memory_mask[None, :], (8, time_count))
-    first_times = step_index[0].astype(jnp.float32) + jnp.arange(row_count, dtype=jnp.int32).astype(
-        jnp.float32
-    )
-    bands = jnp.stack(
-        [
-            band_energy(own_map, (first_times + float(offset)) * TIME_STEP, SIDE)
-            for offset in range(STEPS + 1)
-        ]
-    )
-    bands = jnp.broadcast_to(bands.reshape(-1, 1), (bands.size, time_count))
-    return advance(mom_size, new_rows, bands, mask_rows, tables, history)
 
 
 def solution(mesh):
@@ -579,7 +617,7 @@
 
     def dispatch(new_rows, *others):
         if fits(dict(mesh.shape), new_rows):
-            return fused_body(mesh.shape["mom"], new_rows, *others)
+            return advance(mesh.shape["mom"], new_rows, *others)
         return body(new_rows, *others)
 
     return jax.shard_map(

time: 319 us -> 302 us (0.947)
  Pallas kernels: 308 us -> 296 us
  other arithmetic: 5.07 us -> 0 us
    pallas_call x1, Pallas kernels: 308 us -> 296 us  [advance(): pl.pallas_call(functools.partial(steps_kernel, mom_size), out_shape=jax.S...]
where the time goes in v2:
time: 302 us; the launch traced here: 300 us
  Pallas kernels  296 us (98%)
    pallas_call x1, Pallas kernels, advance(): pl.pallas_call(functools.partial(steps_kernel, mom_size), out_shape=jax.S...  296 us

profile of v2, /device:TPU:26, one launch (start us, length us, event | category | flops | bytes accessed | tf_op | source)
XLA Modules:
  0.0 300.0 jit_solution(16588687955150386307)
XLA Ops:
  1.3 296.5 %advance_rows.1 = f32[2048,128]{1,0:T(8,128)} custom-call(s32[1,256]{1,0:T(1,128)} %bitcast.5, s32[1]{0:T(128)S(6)} %copy.7.step_ref, s32[1]{0:T(128)S(6)} %copy.8.length_ref, f32[2048,128]{1,0:T(8,128)} %bitcast.4, f32[3,2,32,128,512]{4,3,2,1,0:T(8,128)} %history_ref.1), custom_call_target="tpu_custom_call" | custom-call | tf_op jit(solution)/shard_map/advance_rows/pallas_call | solution.py:573
  297.8 2.3 copy.9

commit v3 on v2

--- a/solution.py
+++ b/solution.py
@@ -165,8 +165,8 @@
 
 STEPS = 2
 CORRECTORS = 2
-CORE_LAG = 1
-CHIP_LAG = 3
+CORE_LAG = 2
+CHIP_LAG = 5
 DEPTH = CHIP_LAG + 1
 UNROLL = 4
 RING = 4
@@ -222,7 +222,9 @@
     rounds = STEPS * stages
     quads = own // UNROLL
     resident = own - quads
-    fetches = rounds * groups * quads
+    units = groups * quads
+    halves_of = quads // pieces
+    fetches = rounds * units
 
     def load(index, slot):
         return pltpu.make_async_copy(
@@ -284,22 +286,22 @@
             device_id_type=MESH,
         )
 
-    def core_copy(turn):
+    def core_copy(unit):
         return pltpu.make_async_remote_copy(
-            src_ref=partial.at[turn % DEPTH, :, 1 - core],
-            dst_ref=core_rows.at[turn],
-            send_sem=core_send.at[turn],
-            recv_sem=core_recv.at[turn],
+            src_ref=partial.at[unit % DEPTH, :, 1 - core],
+            dst_ref=core_rows.at[unit],
+            send_sem=core_send.at[unit],
+            recv_sem=core_recv.at[unit],
             device_id={"tm": near},
             device_id_type=MESH,
         )
 
-    def chip_copy(turn):
+    def chip_copy(unit):
         return pltpu.make_async_remote_copy(
-            src_ref=partial.at[turn % DEPTH, 1 - chip, core],
-            dst_ref=chip_rows.at[turn],
-            send_sem=chip_send.at[turn],
-            recv_sem=chip_recv.at[turn],
+            src_ref=partial.at[unit % DEPTH, 1 - chip, core],
+            dst_ref=chip_rows.at[unit],
+            send_sem=chip_send.at[unit],
+            recv_sem=chip_recv.at[unit],
             device_id={"tm": far},
             device_id_type=MESH,
         )
@@ -401,9 +403,9 @@
         for step in range(1, mom_size):
             all_rows(group, step).wait_send()
 
-    def one_momentum(slot, turn, inner):
+    def one_momentum(slot, unit, place):
         depth = 4 * chunk
-        start = turn * mom_size * depth + inner
+        start = unit // halves_of * mom_size * depth + unit % halves_of * UNROLL + place
         ret_re, ret_im, less_re, less_im = [
             returned[pl.ds(start + part * chunk, mom_size, stride=depth), :] for part in range(4)
         ]
@@ -431,16 +433,16 @@
         less_sum = applied(ret_high, ret_both, 1) + applied(less_high, less_both, 2)
         for block in range(4):
             window = slice(block * times, (block + 1) * times)
-            partial[turn % DEPTH, block // 2, block % 2, inner, :lines] = ret_sum[:, window]
-            partial[turn % DEPTH, block // 2, block % 2, inner, lines:] = less_sum[:, window]
-
-    def update(turn, inner, moment, first):
-        group = turn // pieces
-        index = (turn % pieces) * chunk + inner
+            partial[unit % DEPTH, block // 2, block % 2, place, :lines] = ret_sum[:, window]
+            partial[unit % DEPTH, block // 2, block % 2, place, lines:] = less_sum[:, window]
+
+    def update(unit, place, moment, first):
+        group = unit // quads
+        index = unit % quads * UNROLL + place
         total = (
-            partial[turn % DEPTH, chip, core, inner]
-            + core_rows[turn, chip, inner]
-            + chip_rows[turn, inner]
+            partial[unit % DEPTH, chip, core, place]
+            + core_rows[unit, chip, place]
+            + chip_rows[unit, place]
         )
         span = [
             pl.ds(
@@ -476,60 +478,58 @@
         def _(group):
             site_stage(group)
 
-        @pl.loop(0, turns + CHIP_LAG)
-        def _(turn):
-            @pl.when(turn < turns)
+        @pl.loop(0, units + CHIP_LAG)
+        def _(unit):
+            @pl.when(unit < units)
             def _():
-                for step in range(1, mom_size):
-                    energy_copy(turn // pieces, turn % pieces, step).wait_recv()
-
-                @pl.loop(0, chunk // UNROLL)
-                def _(part):
-                    quad = turn % pieces * (chunk // UNROLL) + part
-                    serial = (count * turns + turn) * (chunk // UNROLL) + part
-
-                    @pl.when((count == 0) & (turn < pieces))
-                    def _():
-                        for place in range(UNROLL - 1):
-                            keep(quad, place).wait()
-
-                    fetch(serial).wait()
+                turn = unit // halves_of
+                quad = unit % quads
+                serial = count * units + unit
+
+                @pl.when(unit % halves_of == 0)
+                def _():
+                    for step in range(1, mom_size):
+                        energy_copy(turn // pieces, turn % pieces, step).wait_recv()
+
+                @pl.when((count == 0) & (unit < quads))
+                def _():
                     for place in range(UNROLL - 1):
-                        one_momentum(
-                            quad * (UNROLL - 1) + place, turn, part * UNROLL + place
-                        )
-                    one_momentum(
-                        resident + serial % RING, turn, part * UNROLL + UNROLL - 1
-                    )
-
-                    @pl.when(serial + RING < fetches)
-                    def _():
-                        fetch(serial + RING).start()
-
-                core_copy(turn).start()
-
-            @pl.when((turn >= CORE_LAG) & (turn < turns + CORE_LAG))
+                        keep(quad, place).wait()
+
+                fetch(serial).wait()
+                for place in range(UNROLL - 1):
+                    one_momentum(quad * (UNROLL - 1) + place, unit, place)
+                one_momentum(resident + serial % RING, unit, UNROLL - 1)
+
+                @pl.when(serial + RING < fetches)
+                def _():
+                    fetch(serial + RING).start()
+
+                core_copy(unit).start()
+
+            @pl.when((unit >= CORE_LAG) & (unit < units + CORE_LAG))
             def _():
-                ready = turn - CORE_LAG
+                ready = unit - CORE_LAG
                 core_copy(ready).wait_recv()
                 partial[ready % DEPTH, 1 - chip, core] = (
                     partial[ready % DEPTH, 1 - chip, core] + core_rows[ready, 1 - chip]
                 )
                 chip_copy(ready).start()
 
-            @pl.when(turn >= CHIP_LAG)
+            @pl.when(unit >= CHIP_LAG)
             def _():
-                ready = turn - CHIP_LAG
+                ready = unit - CHIP_LAG
                 chip_copy(ready).wait_recv()
 
-                @pl.loop(0, chunk)
-                def _(inner):
-                    update(ready, inner, moment, first)
-
-                @pl.when(count + 1 < rounds)
+                @pl.loop(0, UNROLL)
+                def _(place):
+                    update(ready, place, moment, first)
+
+                @pl.when((count + 1 < rounds) & (ready % halves_of == halves_of - 1))
                 def _():
-                    publish(ready // pieces, ready % pieces)
-                    send_rows(ready // pieces, ready % pieces)
+                    turn = ready // halves_of
+                    publish(turn // pieces, turn % pieces)
+                    send_rows(turn // pieces, turn % pieces)
 
                 core_copy(ready).wait_send()
                 chip_copy(ready).wait_send()
@@ -560,6 +560,7 @@
     chunk = 8
     pieces = own // chunk
     turns = groups * pieces
+    units = groups * (own // UNROLL)
     slots = own - own // UNROLL + RING
     lines = parts * mom_size
     sites = own * mom_size
@@ -582,9 +583,9 @@
             pltpu.VMEM((groups, mom_size, pieces, parts, chunk, times), f32),
             pltpu.VMEM((groups, mom_size, pieces, parts * chunk, times), f32),
             pltpu.VMEM((turns * mom_size * parts * chunk, times), f32),
-            pltpu.VMEM((DEPTH, 2, 2, chunk, lines, times), f32),
-            pltpu.VMEM((turns, 2, chunk, lines, times), f32),
-            pltpu.VMEM((turns, chunk, lines, times), f32),
+            pltpu.VMEM((DEPTH, 2, 2, UNROLL, lines, times), f32),
+            pltpu.VMEM((units, 2, UNROLL, lines, times), f32),
+            pltpu.VMEM((units, UNROLL, lines, times), f32),
             pltpu.VMEM((slots, 3, 2, times, full), f32),
             table,
             table,
@@ -598,10 +599,10 @@
             dma((groups, mom_size)),
             dma((groups, pieces, mom_size)),
             dma((groups, pieces, mom_size)),
-            dma((turns,)),
-            dma((turns,)),
-            dma((turns,)),
-            dma((turns,)),
+            dma((units,)),
+            dma((units,)),
+            dma((units,)),
+            dma((units,)),
         ],
         compiler_params=pltpu.CompilerParams(
             collective_id=0, has_side_effects=True, vmem_limit_bytes=63 * 1024 * 1024

time: 302 us -> 301 us (level)
  no operation moved by 1% of the time
where the time goes in v3:
time: 301 us
  Pallas kernels  297 us (99%)
    pallas_call x1, Pallas kernels, advance(): pl.pallas_call(functools.partial(steps_kernel, mom_size), out_shape=jax.S...  297 us

profile of v3, /device:TPU:26, one launch (start us, length us, event | category | flops | bytes accessed | tf_op | source)
XLA Modules:
  0.0 300.8 jit_solution(10367383622003208150)
XLA Ops:
  1.3 297.2 %advance_rows.1 = f32[2048,128]{1,0:T(8,128)} custom-call(s32[1,256]{1,0:T(1,128)} %bitcast.5, s32[1]{0:T(128)S(6)} %copy.7.step_ref, s32[1]{0:T(128)S(6)} %copy.8.length_ref, f32[2048,128]{1,0:T(8,128)} %bitcast.4, f32[3,2,32,128,512]{4,3,2,1,0:T(8,128)} %history_ref.1), custom_call_target="tpu_custom_call" | custom-call | tf_op jit(solution)/shard_map/advance_rows/pallas_call | solution.py:574
  298.5 2.3 copy.9
